TPU v7x, 32 devices: a whole 2x2x4 slice. The times are simulated.
32 devices in a mesh: group: 2 (over y), slab: 4 (over z), subj: 2 (over x), yslab: 2 (over core).
Axes of the slice: x: 2, y: 2, z: 4, core: 2. Of those that a mesh axis runs over, the one named last changes fastest.
Arguments:
- subjects: bfloat16 [4, 64, 16, 256], P(('group', 'subj'), 'slab', 'yslab'), parts along dimension 0, may hold values from -6 to 6
- offsets: int32 [4, 3, 64, 16, 256], P(('group', 'subj'), None, 'slab', 'yslab'), parts along dimension 0, may hold values from -2 to 1
- template: float32 [128, 16, 256], P(('group', 'slab'), 'yslab'), parts along dimension 0, may hold values from -6 to 6
- control: float32 [4, 3, 19, 7, 128], P(('group', 'subj')), parts along dimension 0, may hold values from -8 to 8
Outputs:
- template_out: float32 [128, 16, 256], P(('group', 'slab'), 'yslab'), parts along dimension 0
- control_out: float32 [4, 3, 19, 7, 128], P(('group', 'subj')), parts along dimension 0
There are 2 independent parts, one for each index of `group`. A program takes and returns all parts, laid end to end along the dimension named above; each array names one. Nothing has to cross between parts.
All inputs are finite; a program needn't handle non-finite values.
Results may differ from a plain program's by a relative error of at most 0.00065.
Values may be sent and summed in bfloat16 or wider, within the bound.
A program may use at most 64 MiB of HBM per device.

v0:
```python
import jax
import jax.numpy as jnp
from jax import lax
from jax.sharding import PartitionSpec as P

KNOT = 4
KNOT_X = 2
HALO = 2
ITERS = 2
step_length = 0.5
tiny_term = 1e-06


def extended_2(value, sides, width):
    for axis, dim in sides:
        peers, length = (lax.axis_size(axis), value.shape[dim])
        up = [(i, (i + 1) % peers) for i in range(peers - 1)]
        down = [(j, i) for i, j in up]
        last = lax.slice_in_dim(value, length - width, length, axis=dim)
        initial = lax.slice_in_dim(value, 0, width, axis=dim)
        before = lax.ppermute(last, axis, up)
        after = lax.ppermute(initial, axis, down)
        value = jnp.concatenate([before, value, after], axis=dim)
    return value


def shifted(block, axis, distance):
    devices = range(lax.axis_size(axis))
    route = [(i - distance, i) for i in devices if i - distance in devices]
    return lax.ppermute(block, axis, route)


def from_root(value, axis, source):
    kept = jnp.where(lax.axis_index(axis) == source, value, 0).astype(value.dtype)
    return lax.psum(kept, axis)


def basis(positions, columns, spacing, wrap):
    cell = positions // spacing
    frac = (positions - cell * spacing).astype(jnp.float32) / spacing
    weights = [
        (1.0 - frac) ** 3 / 6.0,
        (3.0 * frac**3 - 6.0 * frac**2 + 4.0) / 6.0,
        (-3.0 * frac**3 + 3.0 * frac**2 + 3.0 * frac + 1.0) / 6.0,
        frac**3 / 6.0,
    ]
    index = jnp.arange(columns, dtype=jnp.int32)
    matrix = jnp.zeros((positions.shape[0], columns), jnp.float32)
    for offset in range(4):
        target = cell + offset
        if wrap:
            target = target % columns
        matrix = matrix + jnp.where(
            index[None, :] == target[:, None], weights[offset][:, None], 0.0
        )
    return matrix


def forward_field(coeffs, basis_z, basis_y, basis_x):
    high = lax.Precision.HIGHEST
    first = jnp.einsum("cabg,za->czbg", coeffs, basis_z, precision=high)
    second = jnp.einsum("czbg,yb->czyg", first, basis_y, precision=high)
    return jnp.einsum("czyg,xg->czyx", second, basis_x, precision=high)


def adjoint_field(gradient, basis_z, basis_y, basis_x):
    high = lax.Precision.HIGHEST
    first = jnp.einsum("czyx,xg->czyg", gradient, basis_x, precision=high)
    second = jnp.einsum("czyg,yb->czbg", first, basis_y, precision=high)
    return jnp.einsum("czbg,za->cabg", second, basis_z, precision=high)


def choose(shift_of, table, lead):
    result = table[-HALO + lead]
    for value in range(-HALO + 1, HALO):
        result = jnp.where(shift_of == value, table[value + lead], result)
    return result


def trilinear_local(volume, shifts, fraction, depth, height, width):
    frac_z, frac_y, frac_x = (fraction[0], fraction[1], fraction[2])
    shift_z, shift_y, shift_x = (shifts[0], shifts[1], shifts[2])
    along_y_of = {}
    diff_y_of = {}
    diff_xy_of = {}
    for move_z in range(-HALO, HALO + 1):
        along_x_of = {}
        diff_x_of = {}
        for move_y in range(-HALO, HALO + 1):
            plane = volume[
                move_z + HALO : move_z + HALO + depth, move_y + HALO : move_y + HALO + height, :
            ].astype(jnp.float32)
            columns = {}
            for move_x in range(-HALO, HALO + 1):
                columns[move_x] = plane[:, :, move_x + HALO : move_x + HALO + width]
            low = choose(shift_x, columns, 0)
            high = choose(shift_x, columns, 1)
            along_x_of[move_y] = low * (1.0 - frac_x) + high * frac_x
            diff_x_of[move_y] = high - low
        along_low = choose(shift_y, along_x_of, 0)
        along_high = choose(shift_y, along_x_of, 1)
        diff_low = choose(shift_y, diff_x_of, 0)
        diff_high = choose(shift_y, diff_x_of, 1)
        along_y_of[move_z] = along_low * (1.0 - frac_y) + along_high * frac_y
        diff_y_of[move_z] = along_high - along_low
        diff_xy_of[move_z] = diff_low * (1.0 - frac_y) + diff_high * frac_y
    along_y = [choose(shift_z, along_y_of, 0), choose(shift_z, along_y_of, 1)]
    diff_y = [choose(shift_z, diff_y_of, 0), choose(shift_z, diff_y_of, 1)]
    diff_xy = [choose(shift_z, diff_xy_of, 0), choose(shift_z, diff_xy_of, 1)]
    warped = along_y[0] * (1.0 - frac_z) + along_y[1] * frac_z
    slope_z = along_y[1] - along_y[0]
    slope_y = diff_y[0] * (1.0 - frac_z) + diff_y[1] * frac_z
    slope_x = diff_xy[0] * (1.0 - frac_z) + diff_xy[1] * frac_z
    return (warped, jnp.stack([slope_z, slope_y, slope_x]))


def shards(subjects, offsets, template, control):
    local_subjects = subjects.shape[0]
    depth, height, width = (subjects.shape[1], subjects.shape[2], subjects.shape[3])
    rows_slab = depth // KNOT
    cohort = local_subjects * lax.axis_size("subj")
    extended = extended_2(subjects, (("slab", 1), ("yslab", 2)), HALO)
    extended = jnp.pad(extended, ((0, 0), (0, 0), (0, 0), (HALO, HALO)))
    basis_z = basis(jnp.arange(depth, dtype=jnp.int32), rows_slab + 3, KNOT, False)
    y_start = lax.axis_index("yslab") * height
    basis_y = basis(y_start + jnp.arange(height, dtype=jnp.int32), control.shape[3], KNOT, False)
    basis_x = basis(jnp.arange(width, dtype=jnp.int32), control.shape[4], KNOT_X, True)
    first_row = lax.axis_index("slab") * rows_slab
    current = template
    coeffs_all = control
    for iteration in range(ITERS):
        band_coeffs = lax.dynamic_slice_in_dim(coeffs_all[0], first_row, rows_slab + 3, 1)
        displace = forward_field(band_coeffs, basis_z, basis_y, basis_x)
        tanh_u = jnp.tanh(displace)
        fraction = 0.5 + 0.5 * tanh_u
        warped, slopes = trilinear_local(extended[0], offsets[0], fraction, depth, height, width)
        resid = warped - current
        grad_u = resid[None] * slopes * (1.0 - tanh_u * tanh_u)
        band_list = [adjoint_field(grad_u, basis_z, basis_y, basis_x)]
        band_grid = jnp.stack(band_list)
        current = lax.psum(warped, "subj") / cohort
        band_grid = lax.psum(band_grid.astype(jnp.bfloat16), "yslab").astype(jnp.float32)
        head_rows = band_grid[:, :, :rows_slab]
        tail_part = band_grid[:, :, rows_slab:]
        carried = shifted(tail_part, "slab", 1)
        head_rows = head_rows.at[:, :, :3].add(carried)
        owned = lax.all_gather(head_rows.astype(jnp.bfloat16), "slab", axis=2, tiled=True).astype(
            head_rows.dtype
        )
        last_part = from_root(tail_part, "slab", lax.axis_size("slab") - 1)
        grid = jnp.concatenate([owned, last_part], axis=2)
        lengths = jnp.sqrt(jnp.sum(grid * grid, axis=1))
        peak = jnp.max(lengths, axis=(1, 2, 3))
        coeffs_all = coeffs_all - step_length * grid / (peak[:, None, None, None, None] + tiny_term)
    return (current, coeffs_all)


def solution(mesh):
    in_specs = (
        P(("group", "subj"), "slab", "yslab", None),
        P(("group", "subj"), None, "slab", "yslab", None),
        P(("group", "slab"), "yslab", None),
        P(("group", "subj"), None, None, None, None),
    )
    out_specs = (P(("group", "slab"), "yslab", None), P(("group", "subj"), None, None, None, None))
    return jax.shard_map(shards, mesh=mesh, in_specs=in_specs, out_specs=out_specs, check_vma=False)
```

profile of v0, /device:TPU:0, one launch (start us, length us, event | category | flops | bytes accessed | tf_op | source)
XLA Modules:
  0.0 160.3 jit_solution(13082636263804256856)
XLA Ops:
  7.2 0.7 fusion.363
  7.9 1.3 collective-permute-start.1
  9.2 5.6 %collective-permute-start = (bf16[1,2,8,256]{3,2,1,0:T(8,128)(2,1)S(1)}, bf16[1,2,8,256]{3,2,1,0:T(8,128)(2,1)S(1)}, u32[]{:S(2)}, u32[]{:S(2)}) collective-permute-start(bf16[1,2,8,256]{3,2,1,0:T(8,128)(2,1)S(1)} %get-tuple-element.162), channel_id=1, source_target_pairs={{0,4},{4,8},{8,12},{1,5},{5,9},{9,13},{2,6},{6,10},{10,14},{3,7},{... | collective-permute-start | bytes 24584 | tf_op jit(solution)/shard_map/ppermute | solution.py:21
  15.2 0.9 constant_dynamic-slice_fusion
  16.2 0.4 convolution_bitcast_fusion.3
  16.7 0.4 convolution_bitcast_fusion.1
  17.1 0.4 copy-done.65
  17.6 1.5 collective-permute-start.2
  19.0 1.3 collective-permute-start.3
  20.4 1.5 multiply_add_fusion.1
  22.8 0.6 copy-done.59
  23.7 0.3 fusion.38
  24.2 0.3 fusion.46
  24.6 0.3 fusion.44
  24.9 0.6 copy-done.64
  25.5 3.3 %fusion.335 = (f32[16,8,256]{2,1,0:T(8,128)S(1)}, f32[16,8,256]{2,1,0:T(8,128)}, f32[16,8,256]{2,1,0:T(8,128)S(1)}, f32[16,8,256]{2,1,0:T(8,128)S(1)}, f32[16,8,...) fusion(f32[16,8,256]{2,1,0:T(8,128)S(1)} %copy-done.64, ...), kind=kLoop, calls=%fused_computation.598 | loop fusion | flops 8093696 | bytes 21266432 | tf_op jit(solution)/shard_map/sub | solution.py:137
  30.5 2.9 %add_bitcast_fusion.2 = (f32[1,16,8,256]{3,2,1,0:T(8,128)S(1)}, f32[16,8,256]{2,1,0:T(8,128)}, f32[16,8,256]{2,1,0:T(8,128)}, f32[16,8,256]{2,1,0:T(8,128)}, f32...) fusion(pred[1,1,16,8,256]{4,3,2,1,0:T(8,128)(4,1)S(1)} %get-tup, ...), kind=kLoop, calls=%fused_computation.248 | loop fusion | flops 2654208 | bytes 8454144 | tf_op jit(solution)/shard_map/stack | solution.py:114
  33.4 0.6 copy-done.70
  34.1 0.8 fusion.4
  35.1 0.4 fusion.217
  35.9 4.2 %psum.42 = bf16[1,3,7,7,128]{4,2,3,1,0:T(8,128)(2,1)S(1)} all-reduce(bf16[1,3,7,7,128]{4,2,3,1,0:T(8,128)(2,1)S(1)} %fusion), channel_id=1, replica_groups=mesh['group'=2,'slab'=4,'subj'=2,'yslab'=2] {'yslab'}, use_global_device_ids=true, to_apply=%region_0.1 | all-reduce | flops 18816 | bytes 75264 | tf_op jit(solution)/shard_map/psum | solution.py:142
  40.2 0.6 copy-done.45
  40.8 3.8 %collective-permute-start.4 = (f32[1,3,3,7,128]{4,2,3,1,0:T(4,128)S(1)}, f32[1,3,3,7,128]{4,2,3,1,0:T(4,128)S(1)}, u32[]{:S(2)}, u32[]{:S(2)}) collective-permute-start(f32[1,3,3,7,128]{4,2,3,1,0:T(4,128)S(1)} %slice.1053), channel_id=1, source_target_pairs={{0,4},{4,8},{8,12},{1,5},{5,9},{9,13},{2,6},{6,10},{10,14},{3,7},{... | collective-permute-start | bytes 96776 | tf_op jit(solution)/shard_map/ppermute | solution.py:30
  44.6 17.6 %psum.43 = f32[1,3,3,7,128]{4,2,3,1,0:T(4,128)S(1)} all-reduce(f32[1,3,3,7,128]{4,2,3,1,0:T(4,128)S(1)} %broadcast_select_fusion.1), channel_id=1, replica_groups=mesh['group'=2,'slab'=4,'subj'=2,'yslab'=2] {'slab'}, use_global_device_ids=true, to_apply=%region_1.2 | all-reduce | flops 8064 | bytes 64512 | tf_op jit(solution)/shard_map/psum | solution.py:35
  62.3 0.7 slice-done
  63.2 13.4 %all_gather.6 = bf16[1,3,16,7,128]{4,3,1,0,2:T(8,128)(2,1)S(1)} all-gather(bf16[1,3,4,7,128]{4,3,1,0,2:T(8,128)(2,1)S(1)} %copy.8), channel_id=1, replica_groups=mesh['group'=2,'slab'=4,'subj'=2,'yslab'=2] {'slab'}, dimensions={2}, use_global_device_ids=true | all-gather | bytes 107520 | tf_op jit(solution)/shard_map/all_gather | solution.py:147
  76.6 0.7 fusion.174
  78.1 1.1 copy_subtract_fusion
  79.2 0.4 convolution_bitcast_fusion.2
  79.7 0.4 convolution_bitcast_fusion
  80.2 1.5 multiply_add_fusion
  81.9 3.0 %subtract_bitcast_fusion = (f32[1,16,8,256]{3,2,1,0:T(8,128)}, f32[16,8,256]{2,1,0:T(8,128)S(1)}, f32[16,8,256]{2,1,0:T(8,128)S(1)}, f32[16,8,256]{2,1,0:T(8,128...) fusion(pred[1,1,16,8,256]{4,3,2,1,0:T(8,128)(4,1)S(1)} %get-tup, ...), kind=kLoop, calls=%fused_computation.191 | loop fusion | flops 4227072 | bytes 8716288 | tf_op jit(solution)/shard_map/stack | solution.py:114
  84.9 0.8 add_bitcast_fusion.1
  86.2 0.5 copy-done.47
  87.0 20.5 %all-reduce.4.cloned.1.call-done = (f32[16,8,256]{2,1,0:T(8,128)}, f32[16,8,256]{2,1,0:T(8,128)}) async-done(((f32[16,8,256]{2,1,0:T(8,128)}, f32[16,8,256]{2,1,0:T(8,128)}), (f32[16,8,256]{2,1,0:T(8,128)}, f32[16,8,256]{2,1,0:T(8,128)})) %all-reduce.4.cloned.1.call-update) | async-done | bytes 262160 | tf_op jit(solution)/shard_map/psum | solution.py:141
  107.5 0.9 multiply_subtract_fusion
  108.5 0.6 copy-done.68
  109.1 0.8 fusion.11
  110.1 0.4 fusion.214
  111.0 3.5 %psum.46 = bf16[1,3,7,7,128]{4,2,3,1,0:T(8,128)(2,1)S(1)} all-reduce(bf16[1,3,7,7,128]{4,2,3,1,0:T(8,128)(2,1)S(1)} %fusion.1), channel_id=1, replica_groups=mesh['group'=2,'slab'=4,'subj'=2,'yslab'=2] {'yslab'}, use_global_device_ids=true, to_apply=%region_6.7 | all-reduce | flops 18816 | bytes 75264 | tf_op jit(solution)/shard_map/psum | solution.py:142
  114.5 0.6 copy-done.46
  115.4 0.7 broadcast_multiply_fusion
  116.1 3.4 %collective-permute-start.5 = (f32[1,3,3,7,128]{4,2,3,1,0:T(4,128)S(1)}, f32[1,3,3,7,128]{4,2,3,1,0:T(4,128)S(1)}, u32[]{:S(2)}, u32[]{:S(2)}) collective-permute-start(f32[1,3,3,7,128]{4,2,3,1,0:T(4,128)S(1)} %slice.1059), channel_id=1, source_target_pairs={{0,4},{4,8},{8,12},{1,5},{5,9},{9,13},{2,6},{6,10},{10,14},{3,7},{... | collective-permute-start | bytes 96776 | tf_op jit(solution)/shard_map/ppermute | solution.py:30
  119.5 17.6 %psum.47 = f32[1,3,3,7,128]{4,2,3,1,0:T(4,128)S(1)} all-reduce(f32[1,3,3,7,128]{4,2,3,1,0:T(4,128)S(1)} %broadcast_select_fusion), channel_id=1, replica_groups=mesh['group'=2,'slab'=4,'subj'=2,'yslab'=2] {'slab'}, use_global_device_ids=true, to_apply=%region_7.8 | all-reduce | flops 8064 | bytes 64512 | tf_op jit(solution)/shard_map/psum | solution.py:35
  137.1 0.7 slice-done.1
  138.0 13.2 %all_gather.7 = bf16[1,3,16,7,128]{4,3,1,0,2:T(8,128)(2,1)S(1)} all-gather(bf16[1,3,4,7,128]{4,3,1,0,2:T(8,128)(2,1)S(1)} %copy.12), channel_id=1, replica_groups=mesh['group'=2,'slab'=4,'subj'=2,'yslab'=2] {'slab'}, dimensions={2}, use_global_device_ids=true | all-gather | bytes 107520 | tf_op jit(solution)/shard_map/all_gather | solution.py:147
  151.3 0.6 fusion.173
  152.6 0.9 copy.15
  (328 shorter events, 5.8 us)
Async XLA Ops:
  7.2 100.3 %all-reduce.4.cloned.1.call-start = ((), (), s32[]{:S(2)}) async-start(), calls=%async_computation | async-start | bytes 524288 | tf_op jit(solution)/shard_map/psum | solution.py:141
  7.9 9.6 %collective-permute-start.1 = (bf16[1,2,8,256]{3,2,1,0:T(8,128)(2,1)S(1)}, bf16[1,2,8,256]{3,2,1,0:T(8,128)(2,1)S(1)}, u32[]{:S(2)}, u32[]{:S(2)}) collective-permute-start(bf16[1,2,8,256]{3,2,1,0:T(8,128)(2,1)S(1)} %get-tuple-element.161), channel_id=1, source_target_pairs={{4,0},{8,4},{12,8},{5,1},{9,5},{13,9},{6,2},{10,6},{14,10},{7,3},{... | collective-permute-start | bytes 24584 | tf_op jit(solution)/shard_map/ppermute | solution.py:22
  9.2 7.9 %collective-permute-start = (bf16[1,2,8,256]{3,2,1,0:T(8,128)(2,1)S(1)}, bf16[1,2,8,256]{3,2,1,0:T(8,128)(2,1)S(1)}, u32[]{:S(2)}, u32[]{:S(2)}) collective-permute-start(bf16[1,2,8,256]{3,2,1,0:T(8,128)(2,1)S(1)} %get-tuple-element.162), channel_id=1, source_target_pairs={{0,4},{4,8},{8,12},{1,5},{5,9},{9,13},{2,6},{6,10},{10,14},{3,7},{... | collective-permute-start | bytes 24584 | tf_op jit(solution)/shard_map/ppermute | solution.py:21
  14.8 1.7 %copy-start.109 = (f32[8]{0:T(128)}, f32[8]{0:T(128)S(1)}, u32[]{:S(2)}) copy-start(f32[8]{0:T(128)S(1)} %get-tuple-element.178) | copy-start | bytes 100
  14.8 1.7 %copy-start.112 = (f32[8]{0:T(128)}, f32[8]{0:T(128)S(1)}, u32[]{:S(2)}) copy-start(f32[8]{0:T(128)S(1)} %get-tuple-element.179) | copy-start | bytes 100
  14.9 1.7 %copy-start.116 = (s32[8]{0:T(128)}, s32[8]{0:T(128)S(1)}, u32[]{:S(2)}) copy-start(s32[8]{0:T(128)S(1)} %get-tuple-element.182) | copy-start | bytes 100
  14.9 1.7 %copy-start.120 = (s32[8]{0:T(128)}, s32[8]{0:T(128)S(1)}, u32[]{:S(2)}) copy-start(s32[8]{0:T(128)S(1)} %get-tuple-element.183) | copy-start | bytes 100
  15.1 18.2 %copy-start.66 = (f32[256]{0:T(256)}, f32[256]{0:T(256)S(1)}, u32[]{:S(2)}) copy-start(f32[256]{0:T(256)S(1)} %get-tuple-element.189) | copy-start | bytes 3076
  15.2 5.2 %copy-start.69 = (s32[256]{0:T(256)}, s32[256]{0:T(256)S(1)}, u32[]{:S(2)}) copy-start(s32[256]{0:T(256)S(1)} %get-tuple-element.186) | copy-start | bytes 3076
  15.2 5.2 %copy-start.73 = (s32[256]{0:T(256)}, s32[256]{0:T(256)S(1)}, u32[]{:S(2)}) copy-start(s32[256]{0:T(256)S(1)} %get-tuple-element.187) | copy-start | bytes 3076
  17.1 3.3 %copy-start.77 = (s32[256]{0:T(256)}, s32[256]{0:T(256)S(1)}, u32[]{:S(2)}) copy-start(s32[256]{0:T(256)S(1)} %get-tuple-element.184) | copy-start | bytes 3076
  17.1 3.3 %copy-start.81 = (s32[256]{0:T(256)}, s32[256]{0:T(256)S(1)}, u32[]{:S(2)}) copy-start(s32[256]{0:T(256)S(1)} %get-tuple-element.185) | copy-start | bytes 3076
  17.6 4.3 %collective-permute-start.2 = (bf16[1,20,2,256]{3,2,1,0:T(2,128)(2,1)S(1)}, bf16[1,20,2,256]{3,2,1,0:T(2,128)(2,1)S(1)}, u32[]{:S(2)}, u32[]{:S(2)}) collective-permute-start(bf16[1,20,2,256]{3,2,1,0:T(2,128)(2,1)S(1)} %get-tuple-element.159), channel_id=1, source_target_pairs={{0,1},{2,3},{4,5},{6,7},{8,9},{10,11},{12,13},{14,15},{16,17},{18,... | collective-permute-start | bytes 61448 | tf_op jit(solution)/shard_map/ppermute | solution.py:21
  19.0 3.1 %collective-permute-start.3 = (bf16[1,20,2,256]{3,2,1,0:T(2,128)(2,1)S(1)}, bf16[1,20,2,256]{3,2,1,0:T(2,128)(2,1)S(1)}, u32[]{:S(2)}, u32[]{:S(2)}) collective-permute-start(bf16[1,20,2,256]{3,2,1,0:T(2,128)(2,1)S(1)} %get-tuple-element.160), channel_id=1, source_target_pairs={{1,0},{3,2},{5,4},{7,6},{9,8},{11,10},{13,12},{15,14},{17,16},{19,... | collective-permute-start | bytes 61448 | tf_op jit(solution)/shard_map/ppermute | solution.py:22
  30.5 2.9 %copy-start.57 = (f32[3,16,8,256]{3,2,1,0:T(8,128)S(1)}, f32[3,16,8,256]{3,2,1,0:T(8,128)}, u32[]{:S(2)}) copy-start(f32[3,16,8,256]{3,2,1,0:T(8,128)} %get-tuple-element.164) | copy-start | bytes 1179652
  30.5 2.9 %copy-start.74 = (s32[256]{0:T(256)S(1)}, s32[256]{0:T(256)}, u32[]{:S(2)}) copy-start(s32[256]{0:T(256)} %copy-done.73) | copy-start | bytes 3076
  30.5 2.9 %copy-start.78 = (s32[256]{0:T(256)S(1)}, s32[256]{0:T(256)}, u32[]{:S(2)}) copy-start(s32[256]{0:T(256)} %copy-done.77) | copy-start | bytes 3076
  30.5 2.9 %copy-start.82 = (s32[256]{0:T(256)S(1)}, s32[256]{0:T(256)}, u32[]{:S(2)}) copy-start(s32[256]{0:T(256)} %copy-done.81) | copy-start | bytes 3076
  40.8 21.4 %collective-permute-start.4 = (f32[1,3,3,7,128]{4,2,3,1,0:T(4,128)S(1)}, f32[1,3,3,7,128]{4,2,3,1,0:T(4,128)S(1)}, u32[]{:S(2)}, u32[]{:S(2)}) collective-permute-start(f32[1,3,3,7,128]{4,2,3,1,0:T(4,128)S(1)} %slice.1053), channel_id=1, source_target_pairs={{0,4},{4,8},{8,12},{1,5},{5,9},{9,13},{2,6},{6,10},{10,14},{3,7},{... | collective-permute-start | bytes 96776 | tf_op jit(solution)/shard_map/ppermute | solution.py:30
  78.0 2.1 %copy-start.71 = (s32[256]{0:T(256)S(1)}, s32[256]{0:T(256)}, u32[]{:S(2)}) copy-start(s32[256]{0:T(256)} %copy-done.69) | copy-start | bytes 3076
  78.0 2.1 %copy-start.75 = (s32[256]{0:T(256)S(1)}, s32[256]{0:T(256)}, u32[]{:S(2)}) copy-start(s32[256]{0:T(256)} %copy-done.73) | copy-start | bytes 3076
  78.0 2.1 %copy-start.79 = (s32[256]{0:T(256)S(1)}, s32[256]{0:T(256)}, u32[]{:S(2)}) copy-start(s32[256]{0:T(256)} %copy-done.77) | copy-start | bytes 3076
  78.0 2.1 %copy-start.83 = (s32[256]{0:T(256)S(1)}, s32[256]{0:T(256)}, u32[]{:S(2)}) copy-start(s32[256]{0:T(256)} %copy-done.81) | copy-start | bytes 3076
  78.0 3.7 %copy-start.30 = (f32[16,8,256]{2,1,0:T(8,128)S(1)}, f32[16,8,256]{2,1,0:T(8,128)}, u32[]{:S(2)}) copy-start(f32[16,8,256]{2,1,0:T(8,128)} %copy-done.29) | copy-start | bytes 393220
  78.0 3.7 %copy-start.32 = (f32[16,8,256]{2,1,0:T(8,128)S(1)}, f32[16,8,256]{2,1,0:T(8,128)}, u32[]{:S(2)}) copy-start(f32[16,8,256]{2,1,0:T(8,128)} %copy-done.31) | copy-start | bytes 393220
  78.1 3.7 %copy-start.34 = (f32[16,8,256]{2,1,0:T(8,128)S(1)}, f32[16,8,256]{2,1,0:T(8,128)}, u32[]{:S(2)}) copy-start(f32[16,8,256]{2,1,0:T(8,128)} %copy-done.33) | copy-start | bytes 393220
  78.1 3.7 %copy-start.36 = (f32[16,8,256]{2,1,0:T(8,128)S(1)}, f32[16,8,256]{2,1,0:T(8,128)}, u32[]{:S(2)}) copy-start(f32[16,8,256]{2,1,0:T(8,128)} %copy-done.35) | copy-start | bytes 393220
  78.1 3.7 %copy-start.38 = (f32[16,8,256]{2,1,0:T(8,128)S(1)}, f32[16,8,256]{2,1,0:T(8,128)}, u32[]{:S(2)}) copy-start(f32[16,8,256]{2,1,0:T(8,128)} %copy-done.37) | copy-start | bytes 393220
  79.1 2.6 %copy-start.28 = (f32[16,8,256]{2,1,0:T(8,128)S(1)}, f32[16,8,256]{2,1,0:T(8,128)}, u32[]{:S(2)}) copy-start(f32[16,8,256]{2,1,0:T(8,128)} %copy-done.27) | copy-start | bytes 393220
  79.2 2.6 %copy-start.24 = (f32[16,8,256]{2,1,0:T(8,128)S(1)}, f32[16,8,256]{2,1,0:T(8,128)}, u32[]{:S(2)}) copy-start(f32[16,8,256]{2,1,0:T(8,128)} %copy-done.23) | copy-start | bytes 393220
  79.2 2.6 %copy-start.26 = (f32[16,8,256]{2,1,0:T(8,128)S(1)}, f32[16,8,256]{2,1,0:T(8,128)}, u32[]{:S(2)}) copy-start(f32[16,8,256]{2,1,0:T(8,128)} %copy-done.25) | copy-start | bytes 393220
  79.7 2.2 %copy-start.16 = (f32[16,8,256]{2,1,0:T(8,128)S(1)}, f32[16,8,256]{2,1,0:T(8,128)}, u32[]{:S(2)}) copy-start(f32[16,8,256]{2,1,0:T(8,128)} %copy-done.15) | copy-start | bytes 393220
  79.7 2.2 %copy-start.18 = (f32[16,8,256]{2,1,0:T(8,128)S(1)}, f32[16,8,256]{2,1,0:T(8,128)}, u32[]{:S(2)}) copy-start(f32[16,8,256]{2,1,0:T(8,128)} %copy-done.17) | copy-start | bytes 393220
  79.7 2.2 %copy-start.20 = (f32[16,8,256]{2,1,0:T(8,128)S(1)}, f32[16,8,256]{2,1,0:T(8,128)}, u32[]{:S(2)}) copy-start(f32[16,8,256]{2,1,0:T(8,128)} %copy-done.19) | copy-start | bytes 393220
  79.7 2.2 %copy-start.22 = (f32[16,8,256]{2,1,0:T(8,128)S(1)}, f32[16,8,256]{2,1,0:T(8,128)}, u32[]{:S(2)}) copy-start(f32[16,8,256]{2,1,0:T(8,128)} %copy-done.21) | copy-start | bytes 393220
  80.1 1.7 %copy-start.2 = (f32[16,8,256]{2,1,0:T(8,128)S(1)}, f32[16,8,256]{2,1,0:T(8,128)}, u32[]{:S(2)}) copy-start(f32[16,8,256]{2,1,0:T(8,128)} %copy-done.1) | copy-start | bytes 393220
  80.2 1.7 %copy-start.4 = (f32[16,8,256]{2,1,0:T(8,128)S(1)}, f32[16,8,256]{2,1,0:T(8,128)}, u32[]{:S(2)}) copy-start(f32[16,8,256]{2,1,0:T(8,128)} %copy-done.3) | copy-start | bytes 393220
  80.2 1.7 %copy-start.6 = (f32[16,8,256]{2,1,0:T(8,128)S(1)}, f32[16,8,256]{2,1,0:T(8,128)}, u32[]{:S(2)}) copy-start(f32[16,8,256]{2,1,0:T(8,128)} %copy-done.5) | copy-start | bytes 393220
  80.2 1.7 %copy-start.8 = (f32[16,8,256]{2,1,0:T(8,128)S(1)}, f32[16,8,256]{2,1,0:T(8,128)}, u32[]{:S(2)}) copy-start(f32[16,8,256]{2,1,0:T(8,128)} %copy-done.7) | copy-start | bytes 393220
  80.2 1.7 %copy-start.10 = (f32[16,8,256]{2,1,0:T(8,128)S(1)}, f32[16,8,256]{2,1,0:T(8,128)}, u32[]{:S(2)}) copy-start(f32[16,8,256]{2,1,0:T(8,128)} %copy-done.9) | copy-start | bytes 393220
  86.8 20.7 %copy-start = (f32[16,8,256]{2,1,0:T(8,128)S(1)}, f32[16,8,256]{2,1,0:T(8,128)}, u32[]{:S(2)}) copy-start(f32[16,8,256]{2,1,0:T(8,128)} %get-tuple-element.116) | copy-start | bytes 393220
  86.8 21.6 %copy-start.62 = (f32[1,16,8,256]{3,2,1,0:T(8,128)S(1)}, f32[1,16,8,256]{3,2,1,0:T(8,128)}, u32[]{:S(2)}) copy-start(f32[1,16,8,256]{3,2,1,0:T(8,128)} %get-tuple-element.32) | copy-start | bytes 393220
  86.8 21.6 %copy-start.72 = (s32[256]{0:T(256)S(1)}, s32[256]{0:T(256)}, u32[]{:S(2)}) copy-start(s32[256]{0:T(256)} %copy-done.69) | copy-start | bytes 3076
  86.8 21.7 %copy-start.76 = (s32[256]{0:T(256)S(1)}, s32[256]{0:T(256)}, u32[]{:S(2)}) copy-start(s32[256]{0:T(256)} %copy-done.73) | copy-start | bytes 3076
  86.8 21.7 %copy-start.80 = (s32[256]{0:T(256)S(1)}, s32[256]{0:T(256)}, u32[]{:S(2)}) copy-start(s32[256]{0:T(256)} %copy-done.77) | copy-start | bytes 3076
  86.8 21.7 %copy-start.84 = (s32[256]{0:T(256)S(1)}, s32[256]{0:T(256)}, u32[]{:S(2)}) copy-start(s32[256]{0:T(256)} %copy-done.81) | copy-start | bytes 3076
  87.0 21.5 %copy-start.58 = (f32[3,16,8,256]{3,2,1,0:T(8,128)S(1)}, f32[3,16,8,256]{3,2,1,0:T(8,128)}, u32[]{:S(2)}) copy-start(f32[3,16,8,256]{3,2,1,0:T(8,128)} %get-tuple-element.167) | copy-start | bytes 1179652
  116.1 21.0 %collective-permute-start.5 = (f32[1,3,3,7,128]{4,2,3,1,0:T(4,128)S(1)}, f32[1,3,3,7,128]{4,2,3,1,0:T(4,128)S(1)}, u32[]{:S(2)}, u32[]{:S(2)}) collective-permute-start(f32[1,3,3,7,128]{4,2,3,1,0:T(4,128)S(1)} %slice.1059), channel_id=1, source_target_pairs={{0,4},{4,8},{8,12},{1,5},{5,9},{9,13},{2,6},{6,10},{10,14},{3,7},{... | collective-permute-start | bytes 96776 | tf_op jit(solution)/shard_map/ppermute | solution.py:30
  (101 other events, 104.9 us)
Sparse Core Ops, SparseCore 0:
  85.9 21.5 all-reduce.3
where the time goes:
time: 161 us; the launch traced here: 160 us
  blocking collectives  69.6 us (43%)
  waiting for transfers between devices  20.7 us (13%)
  between operations  17.3 us (11%)
  starting transfers between devices  16.8 us (10%)
  other arithmetic  16.6 us (10%)
  local copies, waits for them, and re-layouts  11.8 us (7%)
  matrix products  7.5 us (5%)
    psum x2, blocking collectives, from_root(): return lax.psum(kept, axis)  35.2 us
    all_gather x2, blocking collectives, shards(): lax.all_gather(head_rows.astype(jnp.bfloat16), 'slab', axis=2, tiled=True)  26.7 us
    psum x1, waiting for transfers between devices, shards(): current = lax.psum(warped, 'subj') / cohort  20.5 us
    unnamed x283, local copies, waits for them, and re-layouts  8.37 us
    psum x2, blocking collectives, shards(): lax.psum(band_grid.astype(jnp.bfloat16), 'yslab').astype(jnp.float32)  7.77 us
    ppermute x2, starting transfers between devices, shifted(): return lax.ppermute(block, axis, route)  7.15 us
    ppermute x2, starting transfers between devices, extended_2(): before = lax.ppermute(last, axis, up)  7.04 us
    another operation x6, other arithmetic, trilinear_local(): return (warped, jnp.stack([slope_z, slope_y, slope_x]))  6.89 us
  transfers between devices with their start and end apart: 7, of which 2 were waited for; matrix products, arithmetic and copies ran while one was open for 2% of the time, Pallas kernels for 0%

commit v1 on v0

--- a/solution.py
+++ b/solution.py
@@ -138,7 +138,7 @@
         grad_u = resid[None] * slopes * (1.0 - tanh_u * tanh_u)
         band_list = [adjoint_field(grad_u, basis_z, basis_y, basis_x)]
         band_grid = jnp.stack(band_list)
-        current = lax.psum(warped, "subj") / cohort
+        current = jnp.sum(lax.all_gather(warped, "subj"), axis=0) / cohort
         band_grid = lax.psum(band_grid.astype(jnp.bfloat16), "yslab").astype(jnp.float32)
         head_rows = band_grid[:, :, :rows_slab]
         tail_part = band_grid[:, :, rows_slab:]

time: 161 us -> 136 us (0.84)
  waiting for transfers between devices: 20.7 us -> 0.23 us
  between operations: 17.3 us -> 3.68 us
  blocking collectives: 69.6 us -> 82.2 us
  starting transfers between devices: 16.8 us -> 14.6 us
  matrix products: 7.5 us -> 9.57 us
  other arithmetic: 16.6 us -> 14.6 us
    psum x1 -> x0, waiting for transfers between devices: 20.5 us -> none  [shards(): current = lax.psum(warped, 'subj') / cohort]
    all_gather x0 -> x2, blocking collectives: none -> 12.6 us  [shards(): current = jnp.sum(lax.all_gather(warped, 'subj'), axis=0) / cohort]
    another operation x6, other arithmetic: 6.89 us -> 2.13 us  [trilinear_local(): return (warped, jnp.stack([slope_z, slope_y, slope_x]))]
    ppermute x2, starting transfers between devices: 7.15 us -> 5.03 us  [shifted(): return lax.ppermute(block, axis, route)]
    unnamed x283 -> x219, local copies, waits for them, and re-layouts: 8.37 us -> 7.24 us
  transfers between devices with their start and end apart: 7 -> 6, of which waited for: 2 -> 1; matrix products, arithmetic and copies ran while one was open for 2% -> 5% of each run, Pallas kernels for 0% -> 0%
where the time goes in v1:
time: 136 us
  blocking collectives  82.2 us (60%)
  starting transfers between devices  14.6 us (11%)
  other arithmetic  14.6 us (11%)
  local copies, waits for them, and re-layouts  10.7 us (8%)
  matrix products  9.57 us (7%)
  between operations  3.68 us (3%)
    psum x2, blocking collectives, from_root(): return lax.psum(kept, axis)  35.1 us
    all_gather x2, blocking collectives, shards(): lax.all_gather(head_rows.astype(jnp.bfloat16), 'slab', axis=2, tiled=True)  26.7 us
    all_gather x2, blocking collectives, shards(): current = jnp.sum(lax.all_gather(warped, 'subj'), axis=0) / cohort  12.6 us
    psum x2, blocking collectives, shards(): lax.psum(band_grid.astype(jnp.bfloat16), 'yslab').astype(jnp.float32)  7.75 us
    unnamed x219, local copies, waits for them, and re-layouts  7.24 us
    ppermute x2, starting transfers between devices, extended_2(): before = lax.ppermute(last, axis, up)  7.04 us
    sub x2, other arithmetic, shards(): resid = warped - current  5.17 us
    ppermute x2, starting transfers between devices, shifted(): return lax.ppermute(block, axis, route)  5.03 us
  transfers between devices with their start and end apart: 6, of which 1 were waited for; matrix products, arithmetic and copies ran while one was open for 5% of the time, Pallas kernels for 0%

profile of v1, /device:TPU:0, one launch (start us, length us, event | category | flops | bytes accessed | tf_op | source)
XLA Modules:
  0.0 135.6 jit_solution(2194223259681769177)
XLA Ops:
  0.6 0.7 fusion.363
  1.3 1.3 collective-permute-start.1
  2.6 5.6 %collective-permute-start = (bf16[1,2,8,256]{3,2,1,0:T(8,128)(2,1)S(1)}, bf16[1,2,8,256]{3,2,1,0:T(8,128)(2,1)S(1)}, u32[]{:S(2)}, u32[]{:S(2)}) collective-permute-start(bf16[1,2,8,256]{3,2,1,0:T(8,128)(2,1)S(1)} %get-tuple-element.159), channel_id=1, source_target_pairs={{0,4},{4,8},{8,12},{1,5},{5,9},{9,13},{2,6},{6,10},{10,14},{3,7},{... | collective-permute-start | bytes 24584 | tf_op jit(solution)/shard_map/ppermute | solution.py:21
  8.5 0.6 fusion.310
  9.1 0.6 and_select_fusion.5
  9.7 0.9 constant_dynamic-slice_fusion
  10.6 1.1 convolution_bitcast_fusion.3
  11.8 0.4 convolution_bitcast_fusion.1
  12.2 0.4 copy-done.65
  12.7 1.5 %collective-permute-start.2 = (bf16[1,20,2,256]{3,2,1,0:T(2,128)(2,1)S(1)}, bf16[1,20,2,256]{3,2,1,0:T(2,128)(2,1)S(1)}, u32[]{:S(2)}, u32[]{:S(2)}) collective-permute-start(bf16[1,20,2,256]{3,2,1,0:T(2,128)(2,1)S(1)} %get-tuple-element.156), channel_id=1, source_target_pairs={{0,1},{2,3},{4,5},{6,7},{8,9},{10,11},{12,13},{14,15},{16,17},{18,... | collective-permute-start | bytes 61448 | tf_op jit(solution)/shard_map/ppermute | solution.py:21
  14.2 1.3 collective-permute-start.3
  15.5 1.6 %multiply_add_fusion.1 = (f32[3,16,8,256]{3,2,1,0:T(8,128)S(1)}, f32[3,16,8,256]{3,2,1,0:T(8,128)}) fusion(f32[3,16,8,128]{3,2,1,0:T(8,128)S(1)} %convolution_bitcast_fusion.1, f32[256]{0:T(256)S(1)} %get-tuple-element.188, s32[256]{0:T(256)S(1)} %get-tuple-element.181, f32[256]{0:T(256)S(1)} %get-tuple-element.187, s32[256]{0:T(256)S(1)} %get-tuple-element.182, ...), kind=kOutput, calls=%fused_computation.32 | convolution fusion | flops 151552000 | bytes 991232 | tf_op jit(solution)/shard_map/czyg,xg->czyx/dot_general | solution.py:63
  17.9 0.7 copy-done.61
  20.0 0.6 copy-done.64
  20.6 2.6 %fusion.335 = (f32[16,8,256]{2,1,0:T(8,128)S(1)}, f32[16,8,256]{2,1,0:T(8,128)S(1)}, f32[16,8,256]{2,1,0:T(8,128)S(1)}, f32[16,8,256]{2,1,0:T(8,128)S(1)}, f32[1...) fusion(f32[16,8,256]{2,1,0:T(8,128)S(1)} %copy-done.64, ...), kind=kLoop, calls=%fused_computation.598 | loop fusion | flops 8093696 | bytes 21266432 | tf_op jit(solution)/shard_map/sub | solution.py:137
  25.2 1.7 %add_bitcast_fusion.2 = (f32[1,16,8,256]{3,2,1,0:T(8,128)S(1)}, f32[16,8,256]{2,1,0:T(8,128)}, f32[16,8,256]{2,1,0:T(8,128)}, f32[16,8,256]{2,1,0:T(8,128)}, f32...) fusion(pred[1,1,16,8,256]{4,3,2,1,0:T(8,128)(4,1)S(1)} %get-tup, ...), kind=kLoop, calls=%fused_computation.248 | loop fusion | flops 2654208 | bytes 8454144 | tf_op jit(solution)/shard_map/stack | solution.py:114
  27.0 0.8 fusion.4
  27.9 0.4 fusion.217
  28.4 0.9 fusion
  29.3 4.2 %psum.28 = bf16[1,3,7,7,128]{4,2,3,1,0:T(8,128)(2,1)S(1)} all-reduce(bf16[1,3,7,7,128]{4,2,3,1,0:T(8,128)(2,1)S(1)} %fusion), channel_id=1, replica_groups=mesh['group'=2,'slab'=4,'subj'=2,'yslab'=2] {'yslab'}, use_global_device_ids=true, to_apply=%region_0.1 | all-reduce | flops 18816 | bytes 75264 | tf_op jit(solution)/shard_map/psum | solution.py:142
  33.6 0.6 copy-done.48
  34.1 6.2 %all-gather.1 = f32[32,8,256]{2,1,0:T(8,128)S(1)} all-gather(f32[16,8,256]{2,1,0:T(8,128)S(1)} %get-tuple-element.45), channel_id=3, replica_groups=mesh['group'=2,'slab'=4,'subj'=2,'yslab'=2] {'subj'}, dimensions={0}, use_global_device_ids=true | all-gather | bytes 393216 | tf_op jit(solution)/shard_map/all_gather | solution.py:141
  40.4 3.7 %collective-permute-start.4 = (f32[1,3,3,7,128]{4,2,3,1,0:T(4,128)S(1)}, f32[1,3,3,7,128]{4,2,3,1,0:T(4,128)S(1)}, u32[]{:S(2)}, u32[]{:S(2)}) collective-permute-start(f32[1,3,3,7,128]{4,2,3,1,0:T(4,128)S(1)} %slice.1053), channel_id=1, source_target_pairs={{0,4},{4,8},{8,12},{1,5},{5,9},{9,13},{2,6},{6,10},{10,14},{3,7},{... | collective-permute-start | bytes 96776 | tf_op jit(solution)/shard_map/ppermute | solution.py:30
  44.2 17.6 %psum.29 = f32[1,3,3,7,128]{4,2,3,1,0:T(4,128)S(1)} all-reduce(f32[1,3,3,7,128]{4,2,3,1,0:T(4,128)S(1)} %broadcast_select_fusion.1), channel_id=1, replica_groups=mesh['group'=2,'slab'=4,'subj'=2,'yslab'=2] {'slab'}, use_global_device_ids=true, to_apply=%region_1.2 | all-reduce | flops 8064 | bytes 64512 | tf_op jit(solution)/shard_map/psum | solution.py:35
  61.8 0.7 reduce_sum.38
  62.5 0.7 slice-done
  63.4 13.4 %all_gather.18 = bf16[1,3,16,7,128]{4,3,1,0,2:T(8,128)(2,1)S(1)} all-gather(bf16[1,3,4,7,128]{4,3,1,0,2:T(8,128)(2,1)S(1)} %copy.8), channel_id=1, replica_groups=mesh['group'=2,'slab'=4,'subj'=2,'yslab'=2] {'slab'}, dimensions={2}, use_global_device_ids=true | all-gather | bytes 107520 | tf_op jit(solution)/shard_map/all_gather | solution.py:147
  76.9 0.7 fusion.174
  78.3 1.1 copy_subtract_fusion
  79.4 0.5 copy-done.77
  80.1 1.1 convolution_bitcast_fusion.2
  81.3 0.4 convolution_bitcast_fusion
  81.9 0.8 multiply_add_fusion
  83.0 2.5 %multiply_subtract_fusion = (f32[16,8,256]{2,1,0:T(8,128)S(1)}, f32[16,8,256]{2,1,0:T(8,128)S(1)}, f32[16,8,256]{2,1,0:T(8,128)S(1)}, f32[16,8,256]{2,1,0:T(8,12...) fusion(f32[16,8,256]{2,1,0:T(8,128)} %reduce_sum.38, ...), kind=kLoop, calls=%fused_computation.192 | loop fusion | flops 4390912 | bytes 9109504 | tf_op jit(solution)/shard_map/sub | solution.py:137
  85.7 0.8 copy-done.50
  86.9 0.8 fusion.11
  87.7 0.4 fusion.214
  88.1 0.9 fusion.1
  89.0 3.5 %psum.30 = bf16[1,3,7,7,128]{4,2,3,1,0:T(8,128)(2,1)S(1)} all-reduce(bf16[1,3,7,7,128]{4,2,3,1,0:T(8,128)(2,1)S(1)} %fusion.1), channel_id=1, replica_groups=mesh['group'=2,'slab'=4,'subj'=2,'yslab'=2] {'yslab'}, use_global_device_ids=true, to_apply=%region_6.7 | all-reduce | flops 18816 | bytes 75264 | tf_op jit(solution)/shard_map/psum | solution.py:142
  92.6 0.6 copy-done.49
  93.2 1.3 collective-permute-start.5
  94.5 6.4 %all-gather = f32[32,8,256]{2,1,0:T(8,128)S(1)} all-gather(f32[16,8,256]{2,1,0:T(8,128)S(1)} %get-tuple-element.31), channel_id=2, replica_groups=mesh['group'=2,'slab'=4,'subj'=2,'yslab'=2] {'subj'}, dimensions={0}, use_global_device_ids=true | all-gather | bytes 393216 | tf_op jit(solution)/shard_map/all_gather | solution.py:141
  100.9 0.7 broadcast_multiply_fusion
  101.6 17.5 %psum.31 = f32[1,3,3,7,128]{4,2,3,1,0:T(4,128)S(1)} all-reduce(f32[1,3,3,7,128]{4,2,3,1,0:T(4,128)S(1)} %broadcast_select_fusion), channel_id=1, replica_groups=mesh['group'=2,'slab'=4,'subj'=2,'yslab'=2] {'slab'}, use_global_device_ids=true, to_apply=%region_7.8 | all-reduce | flops 8064 | bytes 64512 | tf_op jit(solution)/shard_map/psum | solution.py:35
  119.2 0.7 slice-done.1
  120.0 13.3 %all_gather.23 = bf16[1,3,16,7,128]{4,3,1,0,2:T(8,128)(2,1)S(1)} all-gather(bf16[1,3,4,7,128]{4,3,1,0,2:T(8,128)(2,1)S(1)} %copy.12), channel_id=1, replica_groups=mesh['group'=2,'slab'=4,'subj'=2,'yslab'=2] {'slab'}, dimensions={2}, use_global_device_ids=true | all-gather | bytes 107520 | tf_op jit(solution)/shard_map/all_gather | solution.py:147
  133.4 0.6 fusion.173
  134.7 0.9 copy.15
  (265 shorter events, 5.7 us)
Async XLA Ops:
  1.3 11.3 %collective-permute-start.1 = (bf16[1,2,8,256]{3,2,1,0:T(8,128)(2,1)S(1)}, bf16[1,2,8,256]{3,2,1,0:T(8,128)(2,1)S(1)}, u32[]{:S(2)}, u32[]{:S(2)}) collective-permute-start(bf16[1,2,8,256]{3,2,1,0:T(8,128)(2,1)S(1)} %get-tuple-element.158), channel_id=1, source_target_pairs={{4,0},{8,4},{12,8},{5,1},{9,5},{13,9},{6,2},{10,6},{14,10},{7,3},{... | collective-permute-start | bytes 24584 | tf_op jit(solution)/shard_map/ppermute | solution.py:22
  2.6 9.6 %collective-permute-start = (bf16[1,2,8,256]{3,2,1,0:T(8,128)(2,1)S(1)}, bf16[1,2,8,256]{3,2,1,0:T(8,128)(2,1)S(1)}, u32[]{:S(2)}, u32[]{:S(2)}) collective-permute-start(bf16[1,2,8,256]{3,2,1,0:T(8,128)(2,1)S(1)} %get-tuple-element.159), channel_id=1, source_target_pairs={{0,4},{4,8},{8,12},{1,5},{5,9},{9,13},{2,6},{6,10},{10,14},{3,7},{... | collective-permute-start | bytes 24584 | tf_op jit(solution)/shard_map/ppermute | solution.py:21
  8.3 3.4 %copy-start.84 = (f32[8]{0:T(128)}, f32[8]{0:T(128)S(1)}, u32[]{:S(2)}) copy-start(f32[8]{0:T(128)S(1)} %get-tuple-element.175) | copy-start | bytes 100
  8.3 3.4 %copy-start.87 = (f32[8]{0:T(128)}, f32[8]{0:T(128)S(1)}, u32[]{:S(2)}) copy-start(f32[8]{0:T(128)S(1)} %get-tuple-element.176) | copy-start | bytes 100
  8.3 3.4 %copy-start.90 = (s32[8]{0:T(128)}, s32[8]{0:T(128)S(1)}, u32[]{:S(2)}) copy-start(s32[8]{0:T(128)S(1)} %get-tuple-element.179) | copy-start | bytes 100
  8.3 3.4 %copy-start.93 = (s32[8]{0:T(128)}, s32[8]{0:T(128)S(1)}, u32[]{:S(2)}) copy-start(s32[8]{0:T(128)S(1)} %get-tuple-element.180) | copy-start | bytes 100
  8.3 3.4 %copy-start.96 = (s32[8]{0:T(128)}, s32[8]{0:T(128)S(1)}, u32[]{:S(2)}) copy-start(s32[8]{0:T(128)S(1)} %get-tuple-element.167) | copy-start | bytes 100
  8.3 3.4 %copy-start.99 = (s32[8]{0:T(128)}, s32[8]{0:T(128)S(1)}, u32[]{:S(2)}) copy-start(s32[8]{0:T(128)S(1)} %get-tuple-element.168) | copy-start | bytes 100
  8.4 3.4 %copy-start.102 = (f32[8]{0:T(128)}, f32[8]{0:T(128)S(1)}, u32[]{:S(2)}) copy-start(f32[8]{0:T(128)S(1)} %get-tuple-element.169) | copy-start | bytes 100
  8.4 3.4 %copy-start.105 = (f32[8]{0:T(128)}, f32[8]{0:T(128)S(1)}, u32[]{:S(2)}) copy-start(f32[8]{0:T(128)S(1)} %get-tuple-element.170) | copy-start | bytes 100
  8.4 19.9 %copy-start.76 = (s32[16]{0:T(128)}, s32[16]{0:T(128)S(1)}, u32[]{:S(2)}) copy-start(s32[16]{0:T(128)S(1)} %get-tuple-element.177) | copy-start | bytes 196
  8.4 19.9 %copy-start.78 = (s32[16]{0:T(128)}, s32[16]{0:T(128)S(1)}, u32[]{:S(2)}) copy-start(s32[16]{0:T(128)S(1)} %get-tuple-element.178) | copy-start | bytes 196
  8.4 19.9 %copy-start.80 = (f32[16]{0:T(128)}, f32[16]{0:T(128)S(1)}, u32[]{:S(2)}) copy-start(f32[16]{0:T(128)S(1)} %get-tuple-element.173) | copy-start | bytes 196
  8.4 19.9 %copy-start.82 = (f32[16]{0:T(128)}, f32[16]{0:T(128)S(1)}, u32[]{:S(2)}) copy-start(f32[16]{0:T(128)S(1)} %get-tuple-element.174) | copy-start | bytes 196
  9.7 17.2 %copy-start.66 = (f32[256]{0:T(256)}, f32[256]{0:T(256)S(1)}, u32[]{:S(2)}) copy-start(f32[256]{0:T(256)S(1)} %get-tuple-element.186) | copy-start | bytes 3076
  9.7 17.2 %copy-start.68 = (s32[256]{0:T(256)}, s32[256]{0:T(256)S(1)}, u32[]{:S(2)}) copy-start(s32[256]{0:T(256)S(1)} %get-tuple-element.183) | copy-start | bytes 3076
  9.7 17.2 %copy-start.70 = (s32[256]{0:T(256)}, s32[256]{0:T(256)S(1)}, u32[]{:S(2)}) copy-start(s32[256]{0:T(256)S(1)} %get-tuple-element.184) | copy-start | bytes 3076
  12.2 14.7 %copy-start.72 = (s32[256]{0:T(256)}, s32[256]{0:T(256)S(1)}, u32[]{:S(2)}) copy-start(s32[256]{0:T(256)S(1)} %get-tuple-element.181) | copy-start | bytes 3076
  12.2 14.7 %copy-start.74 = (s32[256]{0:T(256)}, s32[256]{0:T(256)S(1)}, u32[]{:S(2)}) copy-start(s32[256]{0:T(256)S(1)} %get-tuple-element.182) | copy-start | bytes 3076
  12.7 4.3 %collective-permute-start.2 = (bf16[1,20,2,256]{3,2,1,0:T(2,128)(2,1)S(1)}, bf16[1,20,2,256]{3,2,1,0:T(2,128)(2,1)S(1)}, u32[]{:S(2)}, u32[]{:S(2)}) collective-permute-start(bf16[1,20,2,256]{3,2,1,0:T(2,128)(2,1)S(1)} %get-tuple-element.156), channel_id=1, source_target_pairs={{0,1},{2,3},{4,5},{6,7},{8,9},{10,11},{12,13},{14,15},{16,17},{18,... | collective-permute-start | bytes 61448 | tf_op jit(solution)/shard_map/ppermute | solution.py:21
  14.2 3.1 %collective-permute-start.3 = (bf16[1,20,2,256]{3,2,1,0:T(2,128)(2,1)S(1)}, bf16[1,20,2,256]{3,2,1,0:T(2,128)(2,1)S(1)}, u32[]{:S(2)}, u32[]{:S(2)}) collective-permute-start(bf16[1,20,2,256]{3,2,1,0:T(2,128)(2,1)S(1)} %get-tuple-element.157), channel_id=1, source_target_pairs={{1,0},{3,2},{5,4},{7,6},{9,8},{11,10},{13,12},{15,14},{17,16},{19,... | collective-permute-start | bytes 61448 | tf_op jit(solution)/shard_map/ppermute | solution.py:22
  25.2 1.8 %copy-start.60 = (f32[3,16,8,256]{3,2,1,0:T(8,128)S(1)}, f32[3,16,8,256]{3,2,1,0:T(8,128)}, u32[]{:S(2)}) copy-start(f32[3,16,8,256]{3,2,1,0:T(8,128)} %get-tuple-element.161) | copy-start | bytes 1179652
  40.4 22.1 %collective-permute-start.4 = (f32[1,3,3,7,128]{4,2,3,1,0:T(4,128)S(1)}, f32[1,3,3,7,128]{4,2,3,1,0:T(4,128)S(1)}, u32[]{:S(2)}, u32[]{:S(2)}) collective-permute-start(f32[1,3,3,7,128]{4,2,3,1,0:T(4,128)S(1)} %slice.1053), channel_id=1, source_target_pairs={{0,4},{4,8},{8,12},{1,5},{5,9},{9,13},{2,6},{6,10},{10,14},{3,7},{... | collective-permute-start | bytes 96776 | tf_op jit(solution)/shard_map/ppermute | solution.py:30
  78.2 3.1 %copy-start.86 = (f32[8]{0:T(128)S(1)}, f32[8]{0:T(128)}, u32[]{:S(2)}) copy-start(f32[8]{0:T(128)} %copy-done.84) | copy-start | bytes 100
  78.2 3.1 %copy-start.89 = (f32[8]{0:T(128)S(1)}, f32[8]{0:T(128)}, u32[]{:S(2)}) copy-start(f32[8]{0:T(128)} %copy-done.87) | copy-start | bytes 100
  78.2 3.1 %copy-start.92 = (s32[8]{0:T(128)S(1)}, s32[8]{0:T(128)}, u32[]{:S(2)}) copy-start(s32[8]{0:T(128)} %copy-done.90) | copy-start | bytes 100
  78.2 3.1 %copy-start.95 = (s32[8]{0:T(128)S(1)}, s32[8]{0:T(128)}, u32[]{:S(2)}) copy-start(s32[8]{0:T(128)} %copy-done.93) | copy-start | bytes 100
  78.2 3.1 %copy-start.98 = (s32[8]{0:T(128)S(1)}, s32[8]{0:T(128)}, u32[]{:S(2)}) copy-start(s32[8]{0:T(128)} %copy-done.96) | copy-start | bytes 100
  78.2 3.1 %copy-start.101 = (s32[8]{0:T(128)S(1)}, s32[8]{0:T(128)}, u32[]{:S(2)}) copy-start(s32[8]{0:T(128)} %copy-done.99) | copy-start | bytes 100
  78.2 3.1 %copy-start.104 = (f32[8]{0:T(128)S(1)}, f32[8]{0:T(128)}, u32[]{:S(2)}) copy-start(f32[8]{0:T(128)} %copy-done.102) | copy-start | bytes 100
  78.2 3.1 %copy-start.107 = (f32[8]{0:T(128)S(1)}, f32[8]{0:T(128)}, u32[]{:S(2)}) copy-start(f32[8]{0:T(128)} %copy-done.105) | copy-start | bytes 100
  78.3 4.4 %copy-start.29 = (f32[16,8,256]{2,1,0:T(8,128)S(1)}, f32[16,8,256]{2,1,0:T(8,128)}, u32[]{:S(2)}) copy-start(f32[16,8,256]{2,1,0:T(8,128)} %copy-done.28) | copy-start | bytes 393220
  78.3 4.4 %copy-start.31 = (f32[16,8,256]{2,1,0:T(8,128)S(1)}, f32[16,8,256]{2,1,0:T(8,128)}, u32[]{:S(2)}) copy-start(f32[16,8,256]{2,1,0:T(8,128)} %copy-done.30) | copy-start | bytes 393220
  78.3 4.4 %copy-start.33 = (f32[16,8,256]{2,1,0:T(8,128)S(1)}, f32[16,8,256]{2,1,0:T(8,128)}, u32[]{:S(2)}) copy-start(f32[16,8,256]{2,1,0:T(8,128)} %copy-done.32) | copy-start | bytes 393220
  78.3 4.4 %copy-start.35 = (f32[16,8,256]{2,1,0:T(8,128)S(1)}, f32[16,8,256]{2,1,0:T(8,128)}, u32[]{:S(2)}) copy-start(f32[16,8,256]{2,1,0:T(8,128)} %copy-done.34) | copy-start | bytes 393220
  78.3 4.4 %copy-start.37 = (f32[16,8,256]{2,1,0:T(8,128)S(1)}, f32[16,8,256]{2,1,0:T(8,128)}, u32[]{:S(2)}) copy-start(f32[16,8,256]{2,1,0:T(8,128)} %copy-done.36) | copy-start | bytes 393220
  79.4 3.3 %copy-start.27 = (f32[16,8,256]{2,1,0:T(8,128)S(1)}, f32[16,8,256]{2,1,0:T(8,128)}, u32[]{:S(2)}) copy-start(f32[16,8,256]{2,1,0:T(8,128)} %copy-done.26) | copy-start | bytes 393220
  80.1 1.7 %copy-start.75 = (s32[256]{0:T(256)S(1)}, s32[256]{0:T(256)}, u32[]{:S(2)}) copy-start(s32[256]{0:T(256)} %copy-done.74) | copy-start | bytes 3076
  80.1 2.6 %copy-start.23 = (f32[16,8,256]{2,1,0:T(8,128)S(1)}, f32[16,8,256]{2,1,0:T(8,128)}, u32[]{:S(2)}) copy-start(f32[16,8,256]{2,1,0:T(8,128)} %copy-done.22) | copy-start | bytes 393220
  80.1 2.6 %copy-start.25 = (f32[16,8,256]{2,1,0:T(8,128)S(1)}, f32[16,8,256]{2,1,0:T(8,128)}, u32[]{:S(2)}) copy-start(f32[16,8,256]{2,1,0:T(8,128)} %copy-done.24) | copy-start | bytes 393220
  83.0 2.6 %copy-start.53 = (f32[16,8,256]{2,1,0:T(8,128)S(1)}, f32[16,8,256]{2,1,0:T(8,128)}, u32[]{:S(2)}) copy-start(f32[16,8,256]{2,1,0:T(8,128)} %get-tuple-element.103) | copy-start | bytes 393220
  83.0 2.6 %copy-start.54 = (f32[16,8,256]{2,1,0:T(8,128)S(1)}, f32[16,8,256]{2,1,0:T(8,128)}, u32[]{:S(2)}) copy-start(f32[16,8,256]{2,1,0:T(8,128)} %get-tuple-element.104) | copy-start | bytes 393220
  83.0 2.7 %copy-start.55 = (f32[16,8,256]{2,1,0:T(8,128)S(1)}, f32[16,8,256]{2,1,0:T(8,128)}, u32[]{:S(2)}) copy-start(f32[16,8,256]{2,1,0:T(8,128)} %get-tuple-element.105) | copy-start | bytes 393220
  83.0 2.7 %copy-start.56 = (f32[16,8,256]{2,1,0:T(8,128)S(1)}, f32[16,8,256]{2,1,0:T(8,128)}, u32[]{:S(2)}) copy-start(f32[16,8,256]{2,1,0:T(8,128)} %get-tuple-element.106) | copy-start | bytes 393220
  83.0 2.7 %copy-start.57 = (f32[16,8,256]{2,1,0:T(8,128)S(1)}, f32[16,8,256]{2,1,0:T(8,128)}, u32[]{:S(2)}) copy-start(f32[16,8,256]{2,1,0:T(8,128)} %get-tuple-element.107) | copy-start | bytes 393220
  83.0 2.7 %copy-start.58 = (f32[16,8,256]{2,1,0:T(8,128)S(1)}, f32[16,8,256]{2,1,0:T(8,128)}, u32[]{:S(2)}) copy-start(f32[16,8,256]{2,1,0:T(8,128)} %get-tuple-element.108) | copy-start | bytes 393220
  83.0 2.7 %copy-start.59 = (f32[16,8,256]{2,1,0:T(8,128)S(1)}, f32[16,8,256]{2,1,0:T(8,128)}, u32[]{:S(2)}) copy-start(f32[16,8,256]{2,1,0:T(8,128)} %get-tuple-element.109) | copy-start | bytes 393220
  93.2 25.9 %collective-permute-start.5 = (f32[1,3,3,7,128]{4,2,3,1,0:T(4,128)S(1)}, f32[1,3,3,7,128]{4,2,3,1,0:T(4,128)S(1)}, u32[]{:S(2)}, u32[]{:S(2)}) collective-permute-start(f32[1,3,3,7,128]{4,2,3,1,0:T(4,128)S(1)} %slice.1059), channel_id=1, source_target_pairs={{0,4},{4,8},{8,12},{1,5},{5,9},{9,13},{2,6},{6,10},{10,14},{3,7},{... | collective-permute-start | bytes 96776 | tf_op jit(solution)/shard_map/ppermute | solution.py:30
  (68 other events, 73.8 us)
